TPU v7x, 32 devices: a whole 2x2x4 slice. The times are simulated.
32 devices in a mesh: section: 2 (over core), group: 4 (over y, x), dp: 4 (over z).
Axes of the slice: x: 2, y: 2, z: 4, core: 2. Of those that a mesh axis runs over, the one named last changes fastest.
Arguments:
- tokens: bfloat16 [2, 4096, 768], P(None, ('group', 'dp')), may hold values from -6 to 6
- cotangent: bfloat16 [2, 4096, 768], P(None, ('group', 'dp')), may hold values from -6 to 6
- lengths: int32 [2, 16, 3], P(None, ('group', 'dp')), may hold values from 1 to 128, 256 in all within a row
- attend_gain: bfloat16 [2, 768], P('section', 'dp'), may hold values from 0.5 to 1.5
- attend_bias: bfloat16 [2, 768], P('section', 'dp'), may hold values from -1.5 to 1.5
- qkv_weight: bfloat16 [2, 768, 2304], P('section', 'dp'), may hold values from -0.21875 to 0.21875
- out_weight: bfloat16 [2, 768, 768], P('section', 'dp'), may hold values from -0.875 to 0.875
- feed_gain: bfloat16 [2, 768], P('section', 'dp'), may hold values from 0.5 to 1.5
- feed_bias: bfloat16 [2, 768], P('section', 'dp'), may hold values from -1.5 to 1.5
- up_weight: bfloat16 [2, 768, 3072], P('section', 'dp'), may hold values from -0.21875 to 0.21875
- down_weight: bfloat16 [2, 3072, 768], P('section', 'dp'), may hold values from -0.109375 to 0.109375
Outputs:
- layer_out: bfloat16 [2, 2, 4096, 768], P('section', None, ('group', 'dp'))
- input_grad: bfloat16 [2, 2, 4096, 768], P('section', None, ('group', 'dp'))
- attend_gain_grad: float32 [2, 768], P('section', 'dp')
- attend_bias_grad: float32 [2, 768], P('section', 'dp')
- qkv_grad: float32 [2, 768, 2304], P('section', 'dp')
- out_grad: float32 [2, 768, 768], P('section', 'dp')
- feed_gain_grad: float32 [2, 768], P('section', 'dp')
- feed_bias_grad: float32 [2, 768], P('section', 'dp')
- up_grad: float32 [2, 768, 3072], P('section', 'dp')
- down_grad: float32 [2, 3072, 768], P('section', 'dp')
Inputs may be any that keep to these rules, and one draw needn't show every extreme that they name: The 3 lengths of one device's block of a micro-batch add up to 256; the longest sequence of every block has 128 tokens.
All inputs are finite; a program needn't handle non-finite values.
Results may differ from a plain program's by a relative error of at most 0.02.
Values may be sent and summed in bfloat16 or wider, within the bound.
No kernel may reach another device: no remote copies, remote signals or barrier semaphores. Data moves between devices by JAX's collectives and lax.ppermute only.
A program may use at most 192 MiB of HBM per device.

v0:
```python
import jax
import jax.numpy as jnp
from jax import lax
from jax.sharding import PartitionSpec as P

HEAD_DIM = 64
masked_score = -1000000000.0


def from_behind(block, axis, distance):
    devices = range(lax.axis_size(axis))
    route = [(i - distance, i) for i in devices if i - distance in devices]
    return lax.ppermute(block, axis, route)


def rope_tables(lengths_row, tok):
    bounds = jnp.cumsum(lengths_row, dtype=jnp.int32)
    places = jnp.arange(tok, dtype=jnp.int32)
    segment = jnp.sum((places[:, None] >= bounds[None, :-1]).astype(jnp.int32), axis=1)
    starts = bounds - lengths_row
    picks = jnp.arange(lengths_row.shape[0], dtype=jnp.int32)
    begin = jnp.sum(jnp.where(segment[:, None] == picks[None, :], starts[None, :], 0), axis=1)
    offset = (places - begin).astype(jnp.float32)
    half = HEAD_DIM // 2
    freqs = 10000.0 ** (-jnp.arange(half, dtype=jnp.float32) / half)
    angles = offset[:, None] * freqs[None, :]
    return (jnp.cos(angles), jnp.sin(angles), segment[:, None] == segment[None, :])


def layer_norm(x, gain, bias):
    center = x - jnp.mean(x, axis=-1, keepdims=True)
    spread = jnp.mean(center * center, axis=-1, keepdims=True)
    return center * lax.rsqrt(spread + 1e-05) * gain + bias


def rotate(heads_in, cosine, sine):
    half = heads_in.shape[-1] // 2
    first = heads_in[..., :half]
    second = heads_in[..., half:]
    cosv = cosine[:, None, :]
    sinv = sine[:, None, :]
    return jnp.concatenate([first * cosv - second * sinv, second * cosv + first * sinv], axis=-1)


def inner(left, right):
    return lax.dot_general(
        left, right, (((0,), (0,)), ((), ())), preferred_element_type=jnp.float32
    )


def times_transposed(left, weight):
    return lax.dot_general(
        left, weight, (((1,), (1,)), ((), ())), preferred_element_type=jnp.float32
    )


def layer_parts(x, weights, tables):
    gain_one, bias_one, qkv_w, out_w, gain_two, bias_two, up_w, down_w = weights
    cosine, sine, same = tables
    tok, width = x.shape
    heads = width // HEAD_DIM
    normed = layer_norm(x, gain_one.astype(jnp.float32), bias_one.astype(jnp.float32)).astype(
        jnp.bfloat16
    )
    qkv = jnp.dot(normed, qkv_w, preferred_element_type=jnp.float32).reshape(
        tok, 3, heads, HEAD_DIM
    )
    query = rotate(qkv[:, 0], cosine, sine).astype(jnp.bfloat16)
    key = rotate(qkv[:, 1], cosine, sine).astype(jnp.bfloat16)
    value = qkv[:, 2].astype(jnp.bfloat16)
    scores = jnp.einsum(
        "qhd,khd->hqk", query, key, preferred_element_type=jnp.float32
    ) * HEAD_DIM ** (-0.5)
    scores = jnp.where(same[None], scores, masked_score)
    peak = jnp.max(scores, axis=-1, keepdims=True)
    expd = jnp.exp(scores - peak)
    probs = expd / jnp.sum(expd, axis=-1, keepdims=True)
    probs_low = probs.astype(jnp.bfloat16)
    mixed = jnp.einsum("hqk,khd->qhd", probs_low, value, preferred_element_type=jnp.float32)
    mixed = mixed.reshape(tok, width).astype(jnp.bfloat16)
    resid = x + jnp.dot(mixed, out_w, preferred_element_type=jnp.float32)
    normed_two = layer_norm(
        resid, gain_two.astype(jnp.float32), bias_two.astype(jnp.float32)
    ).astype(jnp.bfloat16)
    upward = jnp.dot(normed_two, up_w, preferred_element_type=jnp.float32)
    active = jax.nn.gelu(upward, approximate=False).astype(jnp.bfloat16)
    return (normed, query, key, value, probs, probs_low, mixed, resid, normed_two, upward, active)


def layer_forward(x, weights, tables):
    saved = layer_parts(x, weights, tables)
    return saved[7] + jnp.dot(saved[10], weights[7], preferred_element_type=jnp.float32)


def layer_backward(x, upstream, weights, tables):
    gain_one, bias_one, qkv_w, out_w, gain_two, bias_two, up_w, down_w = weights
    cosine, sine, same = tables
    normed, query, key, value, probs, probs_low, mixed, resid, normed_two, upward, active = (
        layer_parts(x, weights, tables)
    )
    tok, width = x.shape
    heads = width // HEAD_DIM
    scale = HEAD_DIM ** (-0.5)
    d_branch_ff = upstream.astype(jnp.bfloat16)
    g_down = inner(active, d_branch_ff)
    d_active = times_transposed(d_branch_ff, down_w)
    _, gelu_pull = jax.vjp(lambda u: jax.nn.gelu(u, approximate=False), upward)
    d_up = gelu_pull(d_active)[0].astype(jnp.bfloat16)
    g_up = inner(normed_two, d_up)
    d_normed_two = times_transposed(d_up, up_w)
    _, norm_pull_two = jax.vjp(
        layer_norm, resid, gain_two.astype(jnp.float32), bias_two.astype(jnp.float32)
    )
    d_resid_part, g_gain_two, g_bias_two = norm_pull_two(d_normed_two)
    d_resid = upstream + d_resid_part
    d_branch = d_resid.astype(jnp.bfloat16)
    g_out = inner(mixed, d_branch)
    d_mixed = times_transposed(d_branch, out_w).astype(jnp.bfloat16).reshape(tok, heads, HEAD_DIM)
    d_value = jnp.einsum("hqk,qhd->khd", probs_low, d_mixed, preferred_element_type=jnp.float32)
    d_probs = jnp.einsum("qhd,khd->hqk", d_mixed, value, preferred_element_type=jnp.float32)
    d_scores = probs * (d_probs - jnp.sum(d_probs * probs, axis=-1, keepdims=True))
    d_scores = d_scores.astype(jnp.bfloat16)
    d_query = jnp.einsum("hqk,khd->qhd", d_scores, key, preferred_element_type=jnp.float32) * scale
    d_key = jnp.einsum("hqk,qhd->khd", d_scores, query, preferred_element_type=jnp.float32) * scale
    d_qkv = jnp.stack(
        [rotate(d_query, cosine, -sine), rotate(d_key, cosine, -sine), d_value], axis=1
    )
    d_qkv = d_qkv.reshape(tok, 3 * width).astype(jnp.bfloat16)
    g_qkv = inner(normed, d_qkv)
    d_normed = times_transposed(d_qkv, qkv_w)
    _, norm_pull_one = jax.vjp(
        layer_norm, x, gain_one.astype(jnp.float32), bias_one.astype(jnp.float32)
    )
    d_x_part, g_gain_one, g_bias_one = norm_pull_one(d_normed)
    d_x = d_resid + d_x_part
    return (d_x, (g_gain_one, g_bias_one, g_qkv, g_out, g_gain_two, g_bias_two, g_up, g_down))


def pick_tables(first, early, late):
    return tuple((jnp.where(first, a, b) for a, b in zip(early, late)))


def on_device(
    tokens,
    cotangent,
    lengths,
    attend_gain,
    attend_bias,
    qkv_weight,
    out_weight,
    feed_gain,
    feed_bias,
    up_weight,
    down_weight,
):
    first = lax.axis_index("section") == 0
    micro = tokens.shape[0]
    tok = tokens.shape[1]
    width = tokens.shape[2]
    shards = (
        attend_gain[0],
        attend_bias[0],
        qkv_weight[0],
        out_weight[0],
        feed_gain[0],
        feed_bias[0],
        up_weight[0],
        down_weight[0],
    )
    weights = (
        lax.all_gather(shards[0], "dp", axis=0, tiled=True),
        lax.all_gather(shards[1], "dp", axis=0, tiled=True),
        lax.all_gather(shards[2], "dp", axis=0, tiled=True),
        lax.all_gather(shards[3], "dp", axis=0, tiled=True),
        lax.all_gather(shards[4], "dp", axis=0, tiled=True),
        lax.all_gather(shards[5], "dp", axis=0, tiled=True),
        lax.all_gather(shards[6], "dp", axis=0, tiled=True),
        lax.all_gather(shards[7], "dp", axis=0, tiled=True),
    )
    tables = [rope_tables(lengths[m, 0], tok) for m in range(micro)]
    received = jnp.zeros((tok, width), jnp.bfloat16)
    inputs = []
    outputs = []
    for tick in range(micro + 1):
        mine = min(tick, micro - 1)
        theirs = max(tick - 1, 0)
        source = jnp.where(first, tokens[mine], received).astype(jnp.float32)
        tabs = pick_tables(first, tables[mine], tables[theirs])
        result = layer_forward(source, weights, tabs).astype(jnp.bfloat16)
        inputs.append(source)
        outputs.append(result)
        if tick < micro:
            received = from_behind(result, "section", 1)
    kept = [jnp.where(first, inputs[m], inputs[m + 1]) for m in range(micro)]
    layer_out = jnp.stack([jnp.where(first, outputs[m], outputs[m + 1]) for m in range(micro)])
    totals = tuple((jnp.zeros(w.shape, jnp.float32) for w in weights))
    received = jnp.zeros((tok, width), jnp.bfloat16)
    sent_back = []
    for tick in range(micro + 1):
        late = min(micro - tick, micro - 1)
        early = max(micro - 1 - tick, 0)
        valid = jnp.where(first, float(tick >= 1), float(tick < micro))
        upstream = jnp.where(first, received, cotangent[early]).astype(jnp.float32)
        source = jnp.where(first, kept[late], kept[early])
        tabs = pick_tables(first, tables[late], tables[early])
        d_x, grads = layer_backward(source, upstream, weights, tabs)
        totals = tuple((total + valid * grad for total, grad in zip(totals, grads)))
        d_low = d_x.astype(jnp.bfloat16)
        sent_back.append(d_low)
        if tick < micro:
            received = from_behind(d_low, "section", -1)
    input_grad = jnp.stack(
        [jnp.where(first, sent_back[micro - m], sent_back[micro - 1 - m]) for m in range(micro)]
    )
    rows = (
        lax.psum_scatter(
            totals[0].astype(jnp.bfloat16), "dp", scatter_dimension=0, tiled=True
        ).astype(jnp.float32),
        lax.psum_scatter(
            totals[1].astype(jnp.bfloat16), "dp", scatter_dimension=0, tiled=True
        ).astype(jnp.float32),
        lax.psum_scatter(
            totals[2].astype(jnp.bfloat16), "dp", scatter_dimension=0, tiled=True
        ).astype(jnp.float32),
        lax.psum_scatter(
            totals[3].astype(jnp.bfloat16), "dp", scatter_dimension=0, tiled=True
        ).astype(jnp.float32),
        lax.psum_scatter(
            totals[4].astype(jnp.bfloat16), "dp", scatter_dimension=0, tiled=True
        ).astype(jnp.float32),
        lax.psum_scatter(
            totals[5].astype(jnp.bfloat16), "dp", scatter_dimension=0, tiled=True
        ).astype(jnp.float32),
        lax.psum_scatter(
            totals[6].astype(jnp.bfloat16), "dp", scatter_dimension=0, tiled=True
        ).astype(jnp.float32),
        lax.psum_scatter(
            totals[7].astype(jnp.bfloat16), "dp", scatter_dimension=0, tiled=True
        ).astype(jnp.float32),
    )
    summed = (
        lax.psum(rows[0].astype(jnp.bfloat16), "group").astype(jnp.float32),
        lax.psum(rows[1].astype(jnp.bfloat16), "group").astype(jnp.float32),
        lax.psum(rows[2].astype(jnp.bfloat16), "group").astype(jnp.float32),
        lax.psum(rows[3].astype(jnp.bfloat16), "group").astype(jnp.float32),
        lax.psum(rows[4].astype(jnp.bfloat16), "group").astype(jnp.float32),
        lax.psum(rows[5].astype(jnp.bfloat16), "group").astype(jnp.float32),
        lax.psum(rows[6].astype(jnp.bfloat16), "group").astype(jnp.float32),
        lax.psum(rows[7].astype(jnp.bfloat16), "group").astype(jnp.float32),
    )
    return (
        layer_out[None],
        input_grad[None],
        summed[0][None],
        summed[1][None],
        summed[2][None],
        summed[3][None],
        summed[4][None],
        summed[5][None],
        summed[6][None],
        summed[7][None],
    )


def solution(mesh):
    placed = (
        P(None, ("group", "dp"), None),
        P(None, ("group", "dp"), None),
        P(None, ("group", "dp"), None),
        P("section", "dp"),
        P("section", "dp"),
        P("section", "dp", None),
        P("section", "dp", None),
        P("section", "dp"),
        P("section", "dp"),
        P("section", "dp", None),
        P("section", "dp", None),
    )
    return jax.shard_map(
        on_device,
        mesh=mesh,
        in_specs=placed,
        out_specs=(
            P("section", None, ("group", "dp"), None),
            P("section", None, ("group", "dp"), None),
            P("section", "dp"),
            P("section", "dp"),
            P("section", "dp", None),
            P("section", "dp", None),
            P("section", "dp"),
            P("section", "dp"),
            P("section", "dp", None),
            P("section", "dp", None),
        ),
        check_vma=False,
    )
```

profile of v0, /device:TPU:0, one launch (start us, length us, event | category | flops | bytes accessed | tf_op | source)
XLA Modules:
  0.0 874.4 jit_solution(11148271096684498808)
XLA Ops:
  12.4 13.9 %all-reduce.9 = (bf16[768]{0:T(1024)(128)(2,1)S(1)}, bf16[768]{0:T(1024)(128)(2,1)S(1)}, bf16[768]{0:T(1024)(128)(2,1)S(1)}, bf16[768]{0:T(1024)(128)(2,1)S(1)}) all-reduce(bf16[768]{0:T(1024)(128)(2,1)S(1)} %dynamic-update-slice.1, bf16[768]{0:T(1024)(128)(2,1)S(1)} %dynamic-update-slice, ...), channel_id=3, replica_groups=mesh['section'=2,'group'=4,'dp'=4] {'dp'}, use_global_device_ids=true, to_apply=%add.1 | all-reduce | flops 3072 | bytes 12288
  29.2 53.3 %all-gather.13.cloned.1.call-done = bf16[1,768,2304]{2,1,0:T(8,128)(2,1)} async-done(((bf16[1,192,2304]{2,1,0:T(8,128)(2,1)}), bf16[1,768,2304]{2,1,0:T(8,128)(2,1)}) %all-gather.13.cloned.1.call-update) | async-done | bytes 3538960 | tf_op jit(solution)/shard_map/all_gather | solution.py:173
  82.5 5.8 copy.96
  88.3 3.4 fusion.365
  94.5 18.6 %all-gather.15.cloned.1.call-done = bf16[1,768,768]{2,1,0:T(8,128)(2,1)} async-done(((bf16[1,192,768]{2,1,0:T(8,128)(2,1)}), bf16[1,768,768]{2,1,0:T(8,128)(2,1)}) %all-gather.15.cloned.1.call-update) | async-done | bytes 1179664 | tf_op jit(solution)/shard_map/all_gather | solution.py:174
  115.2 88.0 %all-gather.19.cloned.1.call-done = bf16[1,3072,768]{2,1,0:T(8,128)(2,1)} async-done(((bf16[1,768,768]{2,1,0:T(8,128)(2,1)}), bf16[1,3072,768]{2,1,0:T(8,128)(2,1)}) %all-gather.19.cloned.1.call-update) | async-done | bytes 4718608 | tf_op jit(solution)/shard_map/all_gather | solution.py:178
  203.3 89.3 %all-gather.17.cloned.1.call-done = bf16[1,768,3072]{2,1,0:T(8,128)(2,1)} async-done(((bf16[1,192,3072]{2,1,0:T(8,128)(2,1)}), bf16[1,768,3072]{2,1,0:T(8,128)(2,1)}) %all-gather.17.cloned.1.call-update) | async-done | bytes 4718608 | tf_op jit(solution)/shard_map/all_gather | solution.py:177
  292.6 12.8 %fusion.287 = bf16[256,768]{1,0:T(8,128)(2,1)S(1)} fusion(f32[256,768]{1,0:T(8,128)S(1)} %get-tuple-element.155, bf16[1,3072,768]{2,1,0:T(8,128)(2,1)} %all-gather.19.cloned.1.call-done, bf16[1,768,3072]{2,1,0:T(8,128)(2,1)} %all-gather.17.cloned.1.call-done, f32[768]{0:T(1024)S(1)} %convert_element_type.462, f32[768]{0:T(1024)S(1)} %convert_element_type.461, ...), kind=kOutput, calls=%fused_computation.351 | convolution fusion | flops 2468413440 | bytes 10625024 | tf_op jit(solution)/shard_map/dot_general | solution.py:92
  309.0 3.7 fusion.48
  317.8 12.8 %fusion.280 = bf16[256,768]{1,0:T(8,128)(2,1)S(1)} fusion(f32[256,768]{1,0:T(8,128)S(1)} %get-tuple-element.159, bf16[1,3072,768]{2,1,0:T(8,128)(2,1)} %all-gather.19.cloned.1.call-done, bf16[1,768,3072]{2,1,0:T(8,128)(2,1)} %all-gather.17.cloned.1.call-done, f32[768]{0:T(1024)S(1)} %convert_element_type.462, f32[768]{0:T(1024)S(1)} %convert_element_type.461, ...), kind=kOutput, calls=%fused_computation.350 | convolution fusion | flops 2468413440 | bytes 10625024 | tf_op jit(solution)/shard_map/dot_general | solution.py:92
  330.6 3.2 collective-permute-start.1
  341.5 4.6 fusion.606
  346.1 2.5 convolution_convert_fusion.8
  349.5 4.6 fusion.28
  354.2 9.8 %add_convert_fusion.5 = bf16[256,3072]{1,0:T(8,128)(2,1)S(1)} fusion(bf16[1,3072,768]{2,1,0:T(8,128)(2,1)S(1)} %bitcast.436, f32[256,3072]{1,0:T(8,128)S(1)} %fusion.28, bf16[2,256,768]{2,1,0:T(8,128)(2,1)S(1)} %copy-done.45, pred[]{:T(512)S(6)} %eq.69), kind=kOutput, calls=%fused_computation.112 | convolution fusion | flops 1264779264 | bytes 9830401 | tf_op jit(solution)/shard_map/dot_general | solution.py:52
  364.0 2.2 multiply_reduce_fusion.5
  371.6 2.7 fusion.294
  383.0 2.2 multiply_reduce_fusion.8
  387.9 3.1 fusion.40
  393.6 4.7 fusion.610
  398.3 2.5 convolution_convert_fusion.5
  410.0 4.6 fusion.612
  414.7 2.6 convolution_convert_fusion.2
  419.0 3.9 fusion.24
  423.1 3.1 fusion.20
  426.2 4.2 fusion.589
  431.5 9.1 %add_convert_fusion.4 = bf16[256,3072]{1,0:T(8,128)(2,1)S(1)} fusion(bf16[256,768]{1,0:T(8,128)(2,1)S(1)} %bitcast_select_fusion.1, bf16[1,3072,768]{2,1,0:T(8,128)(2,1)S(1)} %bitcast.438, f32[256,3072]{1,0:T(8,128)S(1)} %fusion.24), kind=kOutput, calls=%fused_computation.95 | convolution fusion | flops 1264582656 | bytes 9830400 | tf_op jit(solution)/shard_map/dot_general | solution.py:52
  448.1 2.7 fusion.295
  464.0 4.2 fusion.587
  468.4 9.3 %add_convert_fusion.3 = bf16[256,3072]{1,0:T(8,128)(2,1)S(1)} fusion(bf16[256,768]{1,0:T(8,128)(2,1)S(1)} %bitcast_select_fusion, bf16[1,3072,768]{2,1,0:T(8,128)(2,1)S(1)} %bitcast.440, f32[256,3072]{1,0:T(8,128)S(1)} %copy-done.180), kind=kOutput, calls=%fused_computation.78 | convolution fusion | flops 1264582656 | bytes 9830400 | tf_op jit(solution)/shard_map/dot_general | solution.py:52
  482.0 5.1 multiply_reduce_fusion
  488.9 3.5 multiply_convert_fusion.3
  498.6 3.3 add_convert_fusion.2
  503.0 3.1 fusion.586
  507.8 6.2 add_convert_fusion.1
  515.1 9.7 %fusion.127 = f32[3072,768]{1,0:T(8,128)S(1)} fusion(f32[256,3072]{1,0:T(8,128)} %copy-done.179, bf16[2,256,768]{2,1,0:T(8,128)(2,1)S(1)} %copy-done.49, pred[]{:T(512)S(6)} %eq.69), kind=kOutput, calls=%fused_computation.191 | convolution fusion | flops 1259274240 | bytes 12976129 | tf_op jit(solution)/shard_map/dot_general | solution.py:46
  524.9 9.9 %fusion.128 = f32[3072,768]{1,0:T(8,128)} fusion(bf16[256,768]{1,0:T(8,128)(2,1)S(1)} %copy-done.31, f32[256,3072]{1,0:T(8,128)S(1)} %copy-done.183), kind=kOutput, calls=%fused_computation.192 | convolution fusion | flops 1259077632 | bytes 12976128 | tf_op jit(solution)/shard_map/dot_general | solution.py:46
  534.8 11.8 %add_convert_fusion = bf16[3072,768]{1,0:T(8,128)(2,1)} fusion(f32[3072,768]{1,0:T(8,128)} %fusion.128, f32[3072,768]{1,0:T(8,128)S(1)} %fusion.127, bf16[256,768]{1,0:T(8,128)(2,1)S(1)} %copy-done.37, f32[]{:T(128)S(6)} %select_n.198, f32[]{:T(128)S(6)} %select_n.197, f32[256,3072]{1,0:T(8,128)S(1)} %copy-done.181), kind=kOutput, calls=%fused_computation.6 | convolution fusion | flops 1270874112 | bytes 27131912 | tf_op jit(solution)/shard_map/dot_general | solution.py:46
  548.5 3.7 fusion.46
  557.7 27.9 %reduce-scatter.5.cloned.1.call-done = bf16[192,2304]{1,0:T(8,128)(2,1)} async-done(((bf16[768,2304]{1,0:T(8,128)(2,1)}), bf16[192,2304]{1,0:T(8,128)(2,1)}) %reduce-scatter.5.cloned.1.call-update) | async-done | bytes 884752 | tf_op jit(solution)/shard_map/reduce_scatter | solution.py:222
  585.6 87.9 %reduce-scatter.9.cloned.1.call-done = bf16[192,3072]{1,0:T(8,128)(2,1)} async-done(((bf16[768,3072]{1,0:T(8,128)(2,1)}), bf16[192,3072]{1,0:T(8,128)(2,1)}) %reduce-scatter.9.cloned.1.call-update) | async-done | bytes 1179664 | tf_op jit(solution)/shard_map/reduce_scatter | solution.py:234
  673.5 88.1 %reduce-scatter.11.cloned.1.call-done = bf16[768,768]{1,0:T(8,128)(2,1)} async-done(((bf16[3072,768]{1,0:T(8,128)(2,1)}), bf16[768,768]{1,0:T(8,128)(2,1)}) %reduce-scatter.11.cloned.1.call-update) | async-done | bytes 1179664 | tf_op jit(solution)/shard_map/reduce_scatter | solution.py:237
  761.7 13.7 %fusion.314 = bf16[1,256,768]{2,1,0:T(8,128)(2,1)} fusion(bf16[256,768]{1,0:T(8,128)(2,1)} %copy-done.88, f32[256,768]{1,0:T(8,128)S(1)} %copy-done.40, bf16[1,3072,768]{2,1,0:T(8,128)(2,1)} %all-gather.19.cloned.1.call-done, bf16[1,768,3072]{2,1,0:T(8,128)(2,1)} %all-gather.17.cloned.1.call-done, f32[768]{0:T(1024)S(1)} %convert_element_type.462, ...), kind=kOutput, calls=%fused_computation.378 | convolution fusion | flops 2468610048 | bytes 11018241 | tf_op jit(solution)/shard_map/dot_general | solution.py:92
  777.5 4.8 multiply_reduce_fusion.6
  782.4 11.1 %all-reduce.8 = (bf16[768]{0:T(1024)(128)(2,1)S(1)}, bf16[768]{0:T(1024)(128)(2,1)S(1)}, bf16[768]{0:T(1024)(128)(2,1)S(1)}, bf16[768]{0:T(1024)(128)(2,1)S(1)}) all-reduce(bf16[768]{0:T(1024)(128)(2,1)S(1)} %add_convert_fusion.46, ...), channel_id=10, replica_groups=mesh['section'=2,'group'=4,'dp'=4] {'dp'}, use_global_device_ids=true, to_apply=%region_60.61.clone | all-reduce | flops 3072 | bytes 12288
  793.8 10.2 %all-reduce.10 = (bf16[1,192]{1,0:T(2,128)(2,1)S(1)}, bf16[1,192]{1,0:T(2,128)(2,1)S(1)}, bf16[1,192]{1,0:T(2,128)(2,1)S(1)}, bf16[1,192]{1,0:T(2,128)(2,1)S(1)}) all-reduce(bf16[1,192]{1,0:T(2,128)(2,1)S(1)} %broadcast_in_dim.143, ...), channel_id=1, replica_groups=mesh['section'=2,'group'=4,'dp'=4] {'group'}, use_global_device_ids=true, to_apply=%region_61.62 | all-reduce | flops 768 | bytes 3072 | tf_op jit(solution)/shard_map/psum | solution.py:242
  809.8 50.1 %all-reduce.14.cloned.1.call-done = (bf16[1,192,2304]{2,1,0:T(8,128)(2,1)}, bf16[1,192,768]{2,1,0:T(8,128)(2,1)}, bf16[1,192,3072]{2,1,0:T(8,128)(2,1)}, bf16[1,768,768]{2,1,0:T(8,128)(2,1)}) async-done(((bf16[1,192,2304]{2,1,0:T(8,128)(2,1)}, bf16[1,192,768]{2,1,0:T(8,128)(2,1)}, bf16[1,192,3072]{2,1,0:T(8,128)(2,1)}, bf16[1,768,768]{2,1,0:T(8,128)(2,1)}), (bf16[1,192,2304]{2,1,0:T(8,128)(2,1)}, ...) | async-done | bytes 3538960 | tf_op jit(solution)/shard_map/psum | solution.py:244
  860.0 2.6 broadcast_in_dim.148
  (616 shorter events, 115.8 us)
Async XLA Ops:
  7.2 19.1 %copy-start.157 = (s32[2,1,3]{2,1,0:T(1,128)S(1)}, s32[2,1,3]{2,1,0:T(1,128)}, u32[]{:S(2)}) copy-start(s32[2,1,3]{2,1,0:T(1,128)} %param.13) | copy-start | bytes 76
  7.2 19.7 %copy-start.7 = (bf16[2,256,768]{2,1,0:T(8,128)(2,1)S(1)}, bf16[2,256,768]{2,1,0:T(8,128)(2,1)}, u32[]{:S(2)}) copy-start(bf16[2,256,768]{2,1,0:T(8,128)(2,1)} %param.11) | copy-start | bytes 2359300
  7.3 75.3 %all-gather.13.cloned.1.call-start = ((), (), s32[]{:S(2)}) async-start(), calls=%async_computation.8 | async-start | bytes 4423680 | tf_op jit(solution)/shard_map/all_gather | solution.py:173
  8.0 105.1 %all-gather.15.cloned.1.call-start = ((), (), s32[]{:S(2)}) async-start(), calls=%async_computation.9 | async-start | bytes 1474560 | tf_op jit(solution)/shard_map/all_gather | solution.py:174
  8.7 194.5 %all-gather.19.cloned.1.call-start = ((), (), s32[]{:S(2)}) async-start(), calls=%async_computation.11 | async-start | bytes 5898240 | tf_op jit(solution)/shard_map/all_gather | solution.py:178
  9.5 283.1 %all-gather.17.cloned.1.call-start = ((), (), s32[]{:S(2)}) async-start(), calls=%async_computation.10 | async-start | bytes 5898240 | tf_op jit(solution)/shard_map/all_gather | solution.py:177
  10.0 547.7 %reduce-scatter.7.cloned.1.call-start = ((), (), s32[]{:S(2)}) async-start(), calls=%async_computation.5 | async-start | bytes 1474560 | tf_op jit(solution)/shard_map/reduce_scatter | solution.py:225
  28.2 64.5 %copy-start.107 = (pred[256,256]{0,1:T(8,128)(4,1)}, pred[256,256]{0,1:T(8,128)(4,1)S(1)}, u32[]{:S(2)}) copy-start(pred[256,256]{0,1:T(8,128)(4,1)S(1)} %get-tuple-element.145) | copy-start | bytes 196612
  28.2 285.5 %copy-start.108 = (pred[256,256]{0,1:T(8,128)(4,1)}, pred[256,256]{0,1:T(8,128)(4,1)S(1)}, u32[]{:S(2)}) copy-start(pred[256,256]{0,1:T(8,128)(4,1)S(1)} %get-tuple-element.144) | copy-start | bytes 196612
  29.2 62.6 %copy-start.78 = (f32[256,32]{0,1:T(8,128)}, f32[256,32]{0,1:T(8,128)S(1)}, u32[]{:S(2)}) copy-start(f32[256,32]{0,1:T(8,128)S(1)} %get-tuple-element.141) | copy-start | bytes 98308
  29.2 62.6 %copy-start.94 = (f32[256,32]{0,1:T(8,128)}, f32[256,32]{0,1:T(8,128)S(1)}, u32[]{:S(2)}) copy-start(f32[256,32]{0,1:T(8,128)S(1)} %get-tuple-element.140) | copy-start | bytes 98308
  29.2 283.6 %copy-start.81 = (f32[256,32]{0,1:T(8,128)}, f32[256,32]{0,1:T(8,128)S(1)}, u32[]{:S(2)}) copy-start(f32[256,32]{0,1:T(8,128)S(1)} %get-tuple-element.135) | copy-start | bytes 98308
  29.2 283.6 %copy-start.96 = (f32[256,32]{0,1:T(8,128)}, f32[256,32]{0,1:T(8,128)S(1)}, u32[]{:S(2)}) copy-start(f32[256,32]{0,1:T(8,128)S(1)} %get-tuple-element.136) | copy-start | bytes 98308
  305.4 3.2 collective-permute-start
  330.6 3.8 collective-permute-start.1
  335.3 91.0 %copy-start.5 = (bf16[256,768]{1,0:T(8,128)(2,1)}, bf16[256,768]{1,0:T(8,128)(2,1)S(1)}, u32[]{:S(2)}) copy-start(bf16[256,768]{1,0:T(8,128)(2,1)S(1)} %get-tuple-element.61) | copy-start | bytes 1179652
  349.2 17.1 %copy-start.9 = (f32[256,768]{1,0:T(8,128)}, f32[256,768]{1,0:T(8,128)S(1)}, u32[]{:S(2)}) copy-start(f32[256,768]{1,0:T(8,128)S(1)} %get-tuple-element.163) | copy-start | bytes 2359300
  349.2 17.1 %copy-start.121 = (f32[256]{0:T(256)}, f32[256]{0:T(256)S(1)}, u32[]{:S(2)}) copy-start(f32[256]{0:T(256)S(1)} %broadcast_multiply_fusion.4) | copy-start | bytes 3076
  349.4 16.8 %copy-start.132 = (f32[256]{0:T(256)}, f32[256]{0:T(256)S(1)}, u32[]{:S(2)}) copy-start(f32[256]{0:T(256)S(1)} %fusion.453) | copy-start | bytes 3076
  349.5 14.5 %slice-start.10 = ((s8[4718592]{0:T(1024)(128)(4,1)}), s8[4194304]{0:T(1024)(128)(4,1)S(1)}, s32[]{:S(2)}) async-start(s8[4718592]{0:T(1024)(128)(4,1)} %bitcast.441), calls=%async_computation.23 | async-start | bytes 8388608
  354.2 9.8 %copy-start.179 = (f32[256,3072]{1,0:T(8,128)}, f32[256,3072]{1,0:T(8,128)S(1)}, u32[]{:S(2)}) copy-start(f32[256,3072]{1,0:T(8,128)S(1)} %fusion.28) | copy-start | bytes 9437188
  354.2 9.8 %slice-start.11 = ((s8[4718592]{0:T(1024)(128)(4,1)}), s8[524288]{0:T(1024)(128)(4,1)S(1)}, s32[]{:S(2)}) async-start(s8[4718592]{0:T(1024)(128)(4,1)} %bitcast.441), calls=%async_computation.24 | async-start | bytes 1048576
  404.4 26.0 %collective-permute-start.2 = (bf16[256,768]{1,0:T(8,128)(2,1)}, bf16[256,768]{1,0:T(8,128)(2,1)}, u32[]{:S(2)}, u32[]{:S(2)}) collective-permute-start(bf16[256,768]{1,0:T(8,128)(2,1)} %add_convert_fusion.13), channel_id=1, source_target_pairs={{16,0},{17,1},{18,2},{19,3},{20,4},{21,5},{22,6},{23,7},{24,8},{25... | collective-permute-start | bytes 1179656 | tf_op jit(solution)/shard_map/ppermute | solution.py:13
  419.0 12.5 %slice-start.6 = ((s8[4718592]{0:T(1024)(128)(4,1)}), s8[4194304]{0:T(1024)(128)(4,1)S(1)}, s32[]{:S(2)}) async-start(s8[4718592]{0:T(1024)(128)(4,1)} %bitcast.437), calls=%async_computation.19 | async-start | bytes 8388608
  431.5 29.8 %copy-start.30 = (bf16[256,768]{1,0:T(8,128)(2,1)}, bf16[256,768]{1,0:T(8,128)(2,1)S(1)}, u32[]{:S(2)}) copy-start(bf16[256,768]{1,0:T(8,128)(2,1)S(1)} %bitcast_select_fusion.1) | copy-start | bytes 1179652
  462.4 5.8 collective-permute-start.3
  464.0 13.7 %slice-start.14 = ((s8[4718592]{0:T(1024)(128)(4,1)}), s8[524288]{0:T(1024)(128)(4,1)S(1)}, s32[]{:S(2)}) async-start(s8[4718592]{0:T(1024)(128)(4,1)} %bitcast.445), calls=%async_computation.27 | async-start | bytes 1048576
  468.3 11.9 %copy-start.36 = (bf16[256,768]{1,0:T(8,128)(2,1)}, bf16[256,768]{1,0:T(8,128)(2,1)S(1)}, u32[]{:S(2)}) copy-start(bf16[256,768]{1,0:T(8,128)(2,1)S(1)} %bitcast_select_fusion) | copy-start | bytes 1179652
  468.3 9.4 %copy-start.17 = (f32[256,768]{1,0:T(8,128)S(1)}, f32[256,768]{1,0:T(8,128)}, u32[]{:S(2)}) copy-start(f32[256,768]{1,0:T(8,128)} %copy-done.16) | copy-start | bytes 2359300
  488.8 96.9 %reduce-scatter.5.cloned.1.call-start = ((), (), s32[]{:S(2)}) async-start(), calls=%async_computation.4 | async-start | bytes 4423680 | tf_op jit(solution)/shard_map/reduce_scatter | solution.py:222
  501.9 171.6 %reduce-scatter.9.cloned.1.call-start = ((), (), s32[]{:S(2)}) async-start(), calls=%async_computation.6 | async-start | bytes 5898240 | tf_op jit(solution)/shard_map/reduce_scatter | solution.py:234
  514.0 10.8 %copy-start.31 = (bf16[256,768]{1,0:T(8,128)(2,1)S(1)}, bf16[256,768]{1,0:T(8,128)(2,1)}, u32[]{:S(2)}) copy-start(bf16[256,768]{1,0:T(8,128)(2,1)} %copy-done.30) | copy-start | bytes 1179652
  514.0 247.6 %reduce-scatter.11.cloned.1.call-start = ((), (), s32[]{:S(2)}) async-start(), calls=%async_computation.7 | async-start | bytes 5898240 | tf_op jit(solution)/shard_map/reduce_scatter | solution.py:237
  515.1 9.7 %copy-start.183 = (f32[256,3072]{1,0:T(8,128)S(1)}, f32[256,3072]{1,0:T(8,128)}, u32[]{:S(2)}) copy-start(f32[256,3072]{1,0:T(8,128)} %copy-done.182) | copy-start | bytes 9437188
  524.8 10.0 %copy-start.37 = (bf16[256,768]{1,0:T(8,128)(2,1)S(1)}, bf16[256,768]{1,0:T(8,128)(2,1)}, u32[]{:S(2)}) copy-start(bf16[256,768]{1,0:T(8,128)(2,1)} %copy-done.36) | copy-start | bytes 1179652
  524.9 10.0 %copy-start.181 = (f32[256,3072]{1,0:T(8,128)S(1)}, f32[256,3072]{1,0:T(8,128)}, u32[]{:S(2)}) copy-start(f32[256,3072]{1,0:T(8,128)} %fusion.20) | copy-start | bytes 9437188
  546.6 313.3 %all-reduce.14.cloned.1.call-start = ((), (), s32[]{:S(2)}) async-start(), calls=%async_computation.12 | async-start | bytes 7077888 | tf_op jit(solution)/shard_map/psum | solution.py:244
  556.1 205.5 %copy-start.154 = (f32[256]{0:T(256)}, f32[256]{0:T(256)S(1)}, u32[]{:S(2)}) copy-start(f32[256]{0:T(256)S(1)} %broadcast_multiply_fusion.6) | copy-start | bytes 3076
  557.2 204.5 %copy-start.40 = (f32[256,768]{1,0:T(8,128)S(1)}, f32[256,768]{1,0:T(8,128)}, u32[]{:S(2)}) copy-start(f32[256,768]{1,0:T(8,128)} %copy-done.39) | copy-start | bytes 2359300
  761.6 13.7 %copy-start.57 = (bf16[1,256,768]{2,1,0:T(8,128)(2,1)S(1)}, bf16[1,256,768]{2,1,0:T(8,128)(2,1)}, u32[]{:S(2)}) copy-start(bf16[1,256,768]{2,1,0:T(8,128)(2,1)} %select_bitcast_fusion.1) | copy-start | bytes 1179652
  761.6 15.7 %copy-start.8 = (bf16[2,256,768]{2,1,0:T(8,128)(2,1)S(1)}, bf16[2,256,768]{2,1,0:T(8,128)(2,1)}, u32[]{:S(2)}) copy-start(bf16[2,256,768]{2,1,0:T(8,128)(2,1)} %param.11) | copy-start | bytes 2359300
  761.7 15.7 %copy-start.27 = (bf16[256,3,12,64]{0,3,2,1:T(8,128)(2,1)S(1)}, bf16[256,3,12,64]{0,3,2,1:T(8,128)(2,1)}, u32[]{:S(2)}) copy-start(bf16[256,3,12,64]{0,3,2,1:T(8,128)(2,1)} %copy-done.26) | copy-start | bytes 3538948
  761.7 15.7 %copy-start.117 = (f32[256]{0:T(256)S(1)}, f32[256]{0:T(256)}, u32[]{:S(2)}) copy-start(f32[256]{0:T(256)} %copy-done.114) | copy-start | bytes 3076
  777.4 29.5 %copy-start.120 = (f32[256]{0:T(256)S(1)}, f32[256]{0:T(256)}, u32[]{:S(2)}) copy-start(f32[256]{0:T(256)} %copy-done.118) | copy-start | bytes 3076
  777.5 31.1 %copy-start.23 = (f32[256,768]{1,0:T(8,128)S(1)}, f32[256,768]{1,0:T(8,128)}, u32[]{:S(2)}) copy-start(f32[256,768]{1,0:T(8,128)} %copy-done.22) | copy-start | bytes 2359300
  777.5 31.1 %copy-start.38 = (bf16[256,768]{1,0:T(8,128)(2,1)S(1)}, bf16[256,768]{1,0:T(8,128)(2,1)}, u32[]{:S(2)}) copy-start(bf16[256,768]{1,0:T(8,128)(2,1)} %copy-done.36) | copy-start | bytes 1179652
  777.5 31.1 %copy-start.148 = (f32[256]{0:T(256)S(1)}, f32[256]{0:T(256)}, u32[]{:S(2)}) copy-start(f32[256]{0:T(256)} %copy-done.147) | copy-start | bytes 3076
  782.3 26.6 %copy-start.53 = (bf16[1,256,768]{2,1,0:T(8,128)(2,1)S(1)}, bf16[1,256,768]{2,1,0:T(8,128)(2,1)}, u32[]{:S(2)}) copy-start(bf16[1,256,768]{2,1,0:T(8,128)(2,1)} %get-tuple-element.53) | copy-start | bytes 1179652
  (165 other events, 478.4 us)
Sparse Core Ops, SparseCore 0:
  9.7 72.8 all-gather.12
  84.1 29.0 all-gather.14
  114.7 88.5 all-gather.18
  204.7 87.8 all-gather.16
  488.9 29.3 reduce-scatter.6
  520.5 65.0 reduce-scatter.4
  587.9 85.5 reduce-scatter.8
  675.8 85.7 reduce-scatter.10
  765.1 94.8 all-reduce.13
where the time goes:
time: 880 us; the launch traced here: 874 us
  waiting for transfers between devices  508 us (58%)
  matrix products  221 us (25%)
  other arithmetic  45.7 us (5%)
  local copies, waits for them, and re-layouts  37.9 us (4%)
  blocking collectives  35.2 us (4%)
  between operations  18.3 us (2%)
    all_gather x1, waiting for transfers between devices, on_device(): lax.all_gather(shards[6], 'dp', axis=0, tiled=True)  89.3 us
    reduce_scatter x1, waiting for transfers between devices, on_device(): lax.psum_scatter(totals[7].astype(jnp.bfloat16), 'dp', scatter_dimension=...  88.1 us
    all_gather x1, waiting for transfers between devices, on_device(): lax.all_gather(shards[7], 'dp', axis=0, tiled=True)  88 us
    reduce_scatter x1, waiting for transfers between devices, on_device(): lax.psum_scatter(totals[6].astype(jnp.bfloat16), 'dp', scatter_dimension=...  87.9 us
    dot_general x12, matrix products, inner(): lax.dot_general(left, right, (((0,), (0,)), ((), ())), preferred_element_...  59.4 us
    all_gather x1, waiting for transfers between devices, on_device(): lax.all_gather(shards[2], 'dp', axis=0, tiled=True)  53.3 us
    psum x1, waiting for transfers between devices, on_device(): lax.psum(rows[2].astype(jnp.bfloat16), 'group').astype(jnp.float32)  50.1 us
    dot_general x12, matrix products, times_transposed(): lax.dot_general(left, weight, (((1,), (1,)), ((), ())), preferred_element...  46.6 us
  transfers between devices with their start and end apart: 13, of which 10 were waited for; matrix products, arithmetic and copies ran while one was open for 15% of the time, Pallas kernels for 0%

commit v1 on v0

--- a/solution.py
+++ b/solution.py
@@ -5,6 +5,17 @@
 
 HEAD_DIM = 64
 masked_score = -1000000000.0
+
+
+def ring_gather(x, axis, dim):
+    ways = lax.axis_size(axis)
+    pieces = [x]
+    for far in range(1, ways):
+        pieces.append(
+            lax.ppermute(pieces[far - 1], axis, [(d, (d - 1) % ways) for d in range(ways)])
+        )
+    line = jnp.concatenate(pieces, axis=dim)
+    return jnp.roll(line, lax.axis_index(axis) * x.shape[dim], axis=dim)
 
 
 def from_behind(block, axis, distance):
@@ -175,7 +186,7 @@
         lax.all_gather(shards[4], "dp", axis=0, tiled=True),
         lax.all_gather(shards[5], "dp", axis=0, tiled=True),
         lax.all_gather(shards[6], "dp", axis=0, tiled=True),
-        lax.all_gather(shards[7], "dp", axis=0, tiled=True),
+        ring_gather(shards[7], "dp", 0),
     )
     tables = [rope_tables(lengths[m, 0], tok) for m in range(micro)]
     received = jnp.zeros((tok, width), jnp.bfloat16)

time: 880 us -> 854 us (0.970)
  waiting for transfers between devices: 508 us -> 410 us
  blocking collectives: 35.2 us -> 59.5 us
  local copies, waits for them, and re-layouts: 37.9 us -> 54.9 us
  other arithmetic: 45.7 us -> 57.8 us
  starting transfers between devices: 8.44 us -> 17.4 us
    ppermute x0 -> x3, waiting for transfers between devices: none -> 100 us  [ring_gather(): lax.ppermute(pieces[far - 1], axis, [(d, (d - 1) % ways) for d in range(w...]
    all_gather x1 -> x0, waiting for transfers between devices: 88 us -> none  [on_device(): lax.all_gather(shards[7], 'dp', axis=0, tiled=True)]
    all_gather x1, waiting for transfers between devices: 53.3 us -> 0.01 us  [on_device(): lax.all_gather(shards[2], 'dp', axis=0, tiled=True)]
    all_gather x1, waiting for transfers between devices: 89.3 us -> 58.2 us  [on_device(): lax.all_gather(shards[6], 'dp', axis=0, tiled=True)]
    unnamed x2, blocking collectives: 25 us -> 49.2 us
    all_gather x1, waiting for transfers between devices: 18.6 us -> 0.02 us  [on_device(): lax.all_gather(shards[3], 'dp', axis=0, tiled=True)]
    unnamed x413 -> x406, local copies, waits for them, and re-layouts: 26.1 us -> 40.5 us
  transfers between devices with their start and end apart: 13 -> 15, of which waited for: 10 -> 9; matrix products, arithmetic and copies ran while one was open for 15% -> 19% of each run, Pallas kernels for 0% -> 0%
where the time goes in v1:
time: 854 us; the launch traced here: 847 us
  waiting for transfers between devices  410 us (48%)
  matrix products  229 us (27%)
  blocking collectives  59.5 us (7%)
  other arithmetic  57.8 us (7%)
  local copies, waits for them, and re-layouts  54.9 us (6%)
  between operations  18.3 us (2%)
  starting transfers between devices  17.4 us (2%)
    ppermute x3, waiting for transfers between devices, ring_gather(): lax.ppermute(pieces[far - 1], axis, [(d, (d - 1) % ways) for d in range(w...  100 us
    reduce_scatter x1, waiting for transfers between devices, on_device(): lax.psum_scatter(totals[7].astype(jnp.bfloat16), 'dp', scatter_dimension=...  88.1 us
    reduce_scatter x1, waiting for transfers between devices, on_device(): lax.psum_scatter(totals[6].astype(jnp.bfloat16), 'dp', scatter_dimension=...  87.7 us
    dot_general x12, matrix products, inner(): lax.dot_general(left, right, (((0,), (0,)), ((), ())), preferred_element_...  63.3 us
    all_gather x1, waiting for transfers between devices, on_device(): lax.all_gather(shards[6], 'dp', axis=0, tiled=True)  58.2 us
    dot_general x12, matrix products, times_transposed(): lax.dot_general(left, weight, (((1,), (1,)), ((), ())), preferred_element...  51.7 us
    psum x1, waiting for transfers between devices, on_device(): lax.psum(rows[2].astype(jnp.bfloat16), 'group').astype(jnp.float32)  49.8 us
    unnamed x2, blocking collectives  49.2 us
  transfers between devices with their start and end apart: 15, of which 9 were waited for; matrix products, arithmetic and copies ran while one was open for 19% of the time, Pallas kernels for 0%

profile of v1, /device:TPU:0, one launch (start us, length us, event | category | flops | bytes accessed | tf_op | source)
XLA Modules:
  0.0 847.0 jit_solution(6205240477779963054)
XLA Ops:
  8.8 5.1 collective-permute-start
  15.7 53.1 %collective-permute-done = bf16[768,768]{1,0:T(8,128)(2,1)S(1)} collective-permute-done((bf16[768,768]{1,0:T(8,128)(2,1)}, bf16[768,768]{1,0:T(8,128)(2,1)S(1)}, u32[]{:S(2)}, u32[]{:S(2)}) %collective-permute-start) | collective-permute-done | bytes 1179680 | tf_op jit(solution)/shard_map/ppermute | solution.py:15
  73.1 47.1 %collective-permute-done.1 = bf16[768,768]{1,0:T(8,128)(2,1)S(1)} collective-permute-done((bf16[768,768]{1,0:T(8,128)(2,1)S(1)}, bf16[768,768]{1,0:T(8,128)(2,1)S(1)}, u32[]{:S(2)}, u32[]{:S(2)}) %collective-permute-start.1) | collective-permute-done | bytes 1179680 | tf_op jit(solution)/shard_map/ppermute | solution.py:15
  120.2 3.1 collective-permute-start.2
  131.2 38.2 %all-reduce.9 = (bf16[768]{0:T(1024)(128)(2,1)}, bf16[768]{0:T(1024)(128)(2,1)}, bf16[768]{0:T(1024)(128)(2,1)}, bf16[768]{0:T(1024)(128)(2,1)}) all-reduce(bf16[768]{0:T(1024)(128)(2,1)S(1)} %dynamic-update-slice.1, bf16[768]{0:T(1024)(128)(2,1)S(1)} %dynamic-update-slice, ...), channel_id=3, replica_groups=mesh['section'=2,'group'=4,'dp'=4] {'dp'}, use_global_device_ids=true, to_apply=%add.1 | all-reduce | flops 3072 | bytes 12288
  178.7 2.5 constant_dynamic-update-slice_fusion.4
  186.9 5.9 copy.96
  192.8 3.3 fusion.350
  201.4 58.2 %all-gather.15.cloned.1.call-done = bf16[1,768,3072]{2,1,0:T(8,128)(2,1)} async-done(((bf16[1,192,3072]{2,1,0:T(8,128)(2,1)}), bf16[1,768,3072]{2,1,0:T(8,128)(2,1)}) %all-gather.15.cloned.1.call-update) | async-done | bytes 4718608 | tf_op jit(solution)/shard_map/all_gather | solution.py:188
  259.6 13.2 %fusion.262 = bf16[256,768]{1,0:T(8,128)(2,1)S(1)} fusion(f32[256,768]{1,0:T(8,128)S(1)} %get-tuple-element.155, bf16[6144,768]{1,0:T(8,128)(2,1)} %constant_dynamic-update-slice_fusion, s32[]{:T(128)S(6)} %select_n.187, bf16[1,768,3072]{2,1,0:T(8,128)(2,1)} %all-gather.15.cloned.1.call-done, f32[768]{0:T(1024)S(1)} %convert_element_type.462, ...), kind=kOutput, calls=%fused_computation.348 | convolution fusion | flops 2468413440 | bytes 11413508 | tf_op jit(solution)/shard_map/dot_general | solution.py:103
  276.4 3.7 fusion.36
  285.9 13.2 %fusion.257 = bf16[256,768]{1,0:T(8,128)(2,1)S(1)} fusion(f32[256,768]{1,0:T(8,128)S(1)} %get-tuple-element.159, bf16[6144,768]{1,0:T(8,128)(2,1)} %constant_dynamic-update-slice_fusion, s32[]{:T(128)S(6)} %select_n.187, bf16[1,768,3072]{2,1,0:T(8,128)(2,1)} %all-gather.15.cloned.1.call-done, f32[768]{0:T(1024)S(1)} %convert_element_type.462, ...), kind=kOutput, calls=%fused_computation.347 | convolution fusion | flops 2468413440 | bytes 11413508 | tf_op jit(solution)/shard_map/dot_general | solution.py:103
  299.1 3.4 collective-permute-start.4
  310.1 4.6 fusion.597
  314.7 2.5 convolution_convert_fusion.8
  318.1 3.9 fusion.16
  322.1 11.9 %add_convert_fusion.5 = bf16[256,3072]{1,0:T(8,128)(2,1)S(1)} fusion(f32[256,3072]{1,0:T(8,128)S(1)} %fusion.16, bf16[6144,768]{1,0:T(8,128)(2,1)} %constant_dynamic-update-slice_fusion, s32[]{:T(128)S(6)} %select_n.187, bf16[2,256,768]{2,1,0:T(8,128)(2,1)S(1)} %copy-done.45, pred[]{:T(512)S(6)} %eq.72), kind=kOutput, calls=%fused_computation.100 | convolution fusion | flops 1264779264 | bytes 9830405 | tf_op jit(solution)/shard_map/dot_general | solution.py:63
  341.5 2.7 fusion.267
  362.0 4.6 fusion.601
  366.6 2.5 convolution_convert_fusion.5
  378.5 4.6 fusion.603
  383.1 2.6 convolution_convert_fusion.2
  387.4 3.8 fusion.12
  391.4 3.1 fusion.8
  394.5 4.3 fusion.580
  399.9 10.9 %add_convert_fusion.4 = bf16[256,3072]{1,0:T(8,128)(2,1)S(1)} fusion(f32[256,3072]{1,0:T(8,128)S(1)} %fusion.12, bf16[256,768]{1,0:T(8,128)(2,1)S(1)} %bitcast_select_fusion.1, bf16[6144,768]{1,0:T(8,128)(2,1)} %constant_dynamic-update-slice_fusion, s32[]{:T(128)S(6)} %select_n.187), kind=kOutput, calls=%fused_computation.83 | convolution fusion | flops 1264582656 | bytes 9830404 | tf_op jit(solution)/shard_map/dot_general | solution.py:63
  418.3 2.7 fusion.268
  434.3 4.1 fusion.578
  438.5 10.7 %add_convert_fusion.3 = bf16[256,3072]{1,0:T(8,128)(2,1)S(1)} fusion(f32[256,3072]{1,0:T(8,128)S(1)} %copy-done.179, bf16[256,768]{1,0:T(8,128)(2,1)S(1)} %bitcast_select_fusion, bf16[6144,768]{1,0:T(8,128)(2,1)} %constant_dynamic-update-slice_fusion, s32[]{:T(128)S(6)} %select_n.187), kind=kOutput, calls=%fused_computation.66 | convolution fusion | flops 1264582656 | bytes 9830404 | tf_op jit(solution)/shard_map/dot_general | solution.py:63
  454.3 5.3 multiply_reduce_fusion
  461.5 3.5 multiply_convert_fusion.3
  471.3 3.3 add_convert_fusion.2
  475.8 3.1 fusion.577
  479.0 5.1 fusion.579
  484.1 6.5 add_convert_fusion.1
  491.8 9.7 %fusion.112 = f32[3072,768]{1,0:T(8,128)S(1)} fusion(f32[256,3072]{1,0:T(8,128)} %copy-done.178, bf16[2,256,768]{2,1,0:T(8,128)(2,1)S(1)} %copy-done.49, pred[]{:T(512)S(6)} %eq.72), kind=kOutput, calls=%fused_computation.191 | convolution fusion | flops 1259274240 | bytes 12976129 | tf_op jit(solution)/shard_map/dot_general | solution.py:57
  501.5 9.9 %fusion.113 = f32[3072,768]{1,0:T(8,128)} fusion(bf16[256,768]{1,0:T(8,128)(2,1)S(1)} %bitcast_select_fusion.1, f32[256,3072]{1,0:T(8,128)S(1)} %copy-done.182), kind=kOutput, calls=%fused_computation.192 | convolution fusion | flops 1259077632 | bytes 12976128 | tf_op jit(solution)/shard_map/dot_general | solution.py:57
  511.5 11.8 %add_convert_fusion = bf16[3072,768]{1,0:T(8,128)(2,1)} fusion(f32[3072,768]{1,0:T(8,128)} %fusion.113, f32[3072,768]{1,0:T(8,128)S(1)} %fusion.112, bf16[256,768]{1,0:T(8,128)(2,1)S(1)} %copy-done.37, f32[]{:T(128)S(6)} %select_n.213, f32[]{:T(128)S(6)} %select_n.212, f32[256,3072]{1,0:T(8,128)S(1)} %copy-done.180), kind=kOutput, calls=%fused_computation.6 | convolution fusion | flops 1270874112 | bytes 27131912 | tf_op jit(solution)/shard_map/dot_general | solution.py:57
  526.0 3.8 fusion.34
  535.2 22.9 %reduce-scatter.5.cloned.1.call-done = bf16[192,2304]{1,0:T(8,128)(2,1)} async-done(((bf16[768,2304]{1,0:T(8,128)(2,1)}), bf16[192,2304]{1,0:T(8,128)(2,1)}) %reduce-scatter.5.cloned.1.call-update) | async-done | bytes 884752 | tf_op jit(solution)/shard_map/reduce_scatter | solution.py:233
  558.1 87.7 %reduce-scatter.9.cloned.1.call-done = bf16[192,3072]{1,0:T(8,128)(2,1)} async-done(((bf16[768,3072]{1,0:T(8,128)(2,1)}), bf16[192,3072]{1,0:T(8,128)(2,1)}) %reduce-scatter.9.cloned.1.call-update) | async-done | bytes 1179664 | tf_op jit(solution)/shard_map/reduce_scatter | solution.py:245
  645.8 88.1 %reduce-scatter.11.cloned.1.call-done = bf16[768,768]{1,0:T(8,128)(2,1)} async-done(((bf16[3072,768]{1,0:T(8,128)(2,1)}), bf16[768,768]{1,0:T(8,128)(2,1)}) %reduce-scatter.11.cloned.1.call-update) | async-done | bytes 1179664 | tf_op jit(solution)/shard_map/reduce_scatter | solution.py:248
  734.0 14.1 %fusion.299 = bf16[1,256,768]{2,1,0:T(8,128)(2,1)} fusion(bf16[256,768]{1,0:T(8,128)(2,1)} %copy-done.89, f32[256,768]{1,0:T(8,128)S(1)} %copy-done.40, bf16[6144,768]{1,0:T(8,128)(2,1)} %constant_dynamic-update-slice_fusion, s32[]{:T(128)S(6)} %select_n.187, bf16[1,768,3072]{2,1,0:T(8,128)(2,1)} %all-gather.15.cloned.1.call-done, ...), kind=kOutput, calls=%fused_computation.375 | convolution fusion | flops 2468610048 | bytes 11806725 | tf_op jit(solution)/shard_map/dot_general | solution.py:103
  750.1 4.8 multiply_reduce_fusion.6
  755.1 11.1 %all-reduce.8 = (bf16[768]{0:T(1024)(128)(2,1)S(1)}, bf16[768]{0:T(1024)(128)(2,1)S(1)}, bf16[768]{0:T(1024)(128)(2,1)S(1)}, bf16[768]{0:T(1024)(128)(2,1)S(1)}) all-reduce(bf16[768]{0:T(1024)(128)(2,1)S(1)} %add_convert_fusion.46, ...), channel_id=9, replica_groups=mesh['section'=2,'group'=4,'dp'=4] {'dp'}, use_global_device_ids=true, to_apply=%region_60.61.clone | all-reduce | flops 3072 | bytes 12288
  766.5 10.3 %all-reduce.10 = (bf16[1,192]{1,0:T(2,128)(2,1)S(1)}, bf16[1,192]{1,0:T(2,128)(2,1)S(1)}, bf16[1,192]{1,0:T(2,128)(2,1)S(1)}, bf16[1,192]{1,0:T(2,128)(2,1)S(1)}) all-reduce(bf16[1,192]{1,0:T(2,128)(2,1)S(1)} %broadcast_in_dim.143, ...), channel_id=1, replica_groups=mesh['section'=2,'group'=4,'dp'=4] {'group'}, use_global_device_ids=true, to_apply=%region_61.62 | all-reduce | flops 768 | bytes 3072 | tf_op jit(solution)/shard_map/psum | solution.py:253
  782.5 49.8 %all-reduce.14.cloned.1.call-done = (bf16[1,192,2304]{2,1,0:T(8,128)(2,1)}, bf16[1,192,768]{2,1,0:T(8,128)(2,1)}, bf16[1,192,3072]{2,1,0:T(8,128)(2,1)}, bf16[1,768,768]{2,1,0:T(8,128)(2,1)}) async-done(((bf16[1,192,2304]{2,1,0:T(8,128)(2,1)}, bf16[1,192,768]{2,1,0:T(8,128)(2,1)}, bf16[1,192,3072]{2,1,0:T(8,128)(2,1)}, bf16[1,768,768]{2,1,0:T(8,128)(2,1)}), (bf16[1,192,2304]{2,1,0:T(8,128)(2,1)}, ...) | async-done | bytes 3538960 | tf_op jit(solution)/shard_map/psum | solution.py:255
  832.3 2.6 broadcast_in_dim.148
  (610 shorter events, 145.9 us)
Async XLA Ops:
  7.2 119.5 %copy-start.173 = (u32[32]{0:T(128)S(1)}, u32[32]{0:T(128)}, u32[]{:S(2)}) copy-start(u32[32]{0:T(128)} %constant.167) | copy-start | bytes 388
  7.2 168.3 %copy-start.29 = (bf16[1,768,768]{2,1,0:T(8,128)(2,1)S(1)}, bf16[1,768,768]{2,1,0:T(8,128)(2,1)}, u32[]{:S(2)}) copy-start(bf16[1,768,768]{2,1,0:T(8,128)(2,1)} %param.21) | copy-start | bytes 3538948
  7.2 116.6 %copy-start.174 = (bf16[1,192]{1,0:T(2,128)(2,1)S(1)}, bf16[1,192]{1,0:T(2,128)(2,1)}, u32[]{:S(2)}) copy-start(bf16[1,192]{1,0:T(2,128)(2,1)} %param.15) | copy-start | bytes 1156
  7.2 117.2 %copy-start.175 = (bf16[1,192]{1,0:T(2,128)(2,1)S(1)}, bf16[1,192]{1,0:T(2,128)(2,1)}, u32[]{:S(2)}) copy-start(bf16[1,192]{1,0:T(2,128)(2,1)} %param.14) | copy-start | bytes 1156
  7.2 117.7 %copy-start.176 = (bf16[1,192]{1,0:T(2,128)(2,1)S(1)}, bf16[1,192]{1,0:T(2,128)(2,1)}, u32[]{:S(2)}) copy-start(bf16[1,192]{1,0:T(2,128)(2,1)} %param.19) | copy-start | bytes 1156
  7.2 179.7 %all-gather.11.cloned.1.call-start = ((), (), s32[]{:S(2)}) async-start(), calls=%async_computation.8 | async-start | bytes 4423680 | tf_op jit(solution)/shard_map/all_gather | solution.py:184
  8.0 191.3 %all-gather.13.cloned.1.call-start = ((), (), s32[]{:S(2)}) async-start(), calls=%async_computation.9 | async-start | bytes 1474560 | tf_op jit(solution)/shard_map/all_gather | solution.py:185
  8.7 250.9 %all-gather.15.cloned.1.call-start = ((), (), s32[]{:S(2)}) async-start(), calls=%async_computation.10 | async-start | bytes 5898240 | tf_op jit(solution)/shard_map/all_gather | solution.py:188
  8.8 60.1 %collective-permute-start = (bf16[768,768]{1,0:T(8,128)(2,1)}, bf16[768,768]{1,0:T(8,128)(2,1)S(1)}, u32[]{:S(2)}, u32[]{:S(2)}) collective-permute-start(bf16[768,768]{1,0:T(8,128)(2,1)} %bitcast.368), channel_id=1, source_target_pairs={{0,3},{1,0},{2,1},{3,2},{4,7},{5,4},{6,5},{7,6},{8,11},{9,8},{10,9... | collective-permute-start | bytes 3538952 | tf_op jit(solution)/shard_map/ppermute | solution.py:15
  13.9 521.4 %reduce-scatter.7.cloned.1.call-start = ((), (), s32[]{:S(2)}) async-start(), calls=%async_computation.5 | async-start | bytes 1474560 | tf_op jit(solution)/shard_map/reduce_scatter | solution.py:236
  15.1 53.9 %copy-start.134 = (s32[256]{0:T(256)}, s32[256]{0:T(256)S(1)}, u32[]{:S(2)}) copy-start(s32[256]{0:T(256)S(1)} %fusion.436) | copy-start | bytes 3076
  68.8 51.3 %collective-permute-start.1 = (bf16[768,768]{1,0:T(8,128)(2,1)S(1)}, bf16[768,768]{1,0:T(8,128)(2,1)S(1)}, u32[]{:S(2)}, u32[]{:S(2)}) collective-permute-start(bf16[768,768]{1,0:T(8,128)(2,1)S(1)} %collective-permute-done), channel_id=1, source_target_pairs={{0,3},{1,0},{2,1},{3,2},{4,7},{5,4},{6,5},{7,6},{8,11},{9,8},{10,9... | collective-permute-start | bytes 3538952 | tf_op jit(solution)/shard_map/ppermute | solution.py:15
  70.7 49.5 %copy-start.139 = (f32[256]{0:T(256)}, f32[256]{0:T(256)S(1)}, u32[]{:S(2)}) copy-start(f32[256]{0:T(256)S(1)} %broadcast_multiply_fusion.11) | copy-start | bytes 3076
  120.2 58.5 %collective-permute-start.2 = (bf16[768,768]{1,0:T(8,128)(2,1)S(1)}, bf16[768,768]{1,0:T(8,128)(2,1)}, u32[]{:S(2)}, u32[]{:S(2)}) collective-permute-start(bf16[768,768]{1,0:T(8,128)(2,1)S(1)} %collective-permute-done.1), channel_id=1, source_target_pairs={{0,3},{1,0},{2,1},{3,2},{4,7},{5,4},{6,5},{7,6},{8,11},{9,8},{10,9... | collective-permute-start | bytes 3538952 | tf_op jit(solution)/shard_map/ppermute | solution.py:15
  272.8 3.2 collective-permute-start.3
  299.1 3.8 collective-permute-start.4
  303.8 90.7 %copy-start.5 = (bf16[256,768]{1,0:T(8,128)(2,1)}, bf16[256,768]{1,0:T(8,128)(2,1)S(1)}, u32[]{:S(2)}) copy-start(bf16[256,768]{1,0:T(8,128)(2,1)S(1)} %get-tuple-element.63) | copy-start | bytes 1179652
  317.8 18.4 %copy-start.8 = (f32[256,768]{1,0:T(8,128)}, f32[256,768]{1,0:T(8,128)S(1)}, u32[]{:S(2)}) copy-start(f32[256,768]{1,0:T(8,128)S(1)} %get-tuple-element.163) | copy-start | bytes 2359300
  317.8 18.4 %copy-start.121 = (f32[256]{0:T(256)}, f32[256]{0:T(256)S(1)}, u32[]{:S(2)}) copy-start(f32[256]{0:T(256)S(1)} %broadcast_multiply_fusion.4) | copy-start | bytes 3076
  318.0 18.1 %copy-start.131 = (f32[256]{0:T(256)}, f32[256]{0:T(256)S(1)}, u32[]{:S(2)}) copy-start(f32[256]{0:T(256)S(1)} %fusion.438) | copy-start | bytes 3076
  318.1 15.9 %slice-start.4 = ((s8[4718592]{0:T(1024)(128)(4,1)}), s8[4194304]{0:T(1024)(128)(4,1)S(1)}, s32[]{:S(2)}) async-start(s8[4718592]{0:T(1024)(128)(4,1)} %bitcast.395), calls=%async_computation.16 | async-start | bytes 8388608
  322.0 11.9 %copy-start.178 = (f32[256,3072]{1,0:T(8,128)}, f32[256,3072]{1,0:T(8,128)S(1)}, u32[]{:S(2)}) copy-start(f32[256,3072]{1,0:T(8,128)S(1)} %fusion.16) | copy-start | bytes 9437188
  322.1 11.9 %slice-start.5 = ((s8[4718592]{0:T(1024)(128)(4,1)}), s8[524288]{0:T(1024)(128)(4,1)S(1)}, s32[]{:S(2)}) async-start(s8[4718592]{0:T(1024)(128)(4,1)} %bitcast.395), calls=%async_computation.17 | async-start | bytes 1048576
  372.8 26.0 %collective-permute-start.5 = (bf16[256,768]{1,0:T(8,128)(2,1)}, bf16[256,768]{1,0:T(8,128)(2,1)}, u32[]{:S(2)}, u32[]{:S(2)}) collective-permute-start(bf16[256,768]{1,0:T(8,128)(2,1)} %add_convert_fusion.13), channel_id=1, source_target_pairs={{16,0},{17,1},{18,2},{19,3},{20,4},{21,5},{22,6},{23,7},{24,8},{25... | collective-permute-start | bytes 1179656 | tf_op jit(solution)/shard_map/ppermute | solution.py:24
  383.1 8.1 slice-start.6
  391.3 8.5 %copy-start.181 = (f32[256,3072]{1,0:T(8,128)}, f32[256,3072]{1,0:T(8,128)S(1)}, u32[]{:S(2)}) copy-start(f32[256,3072]{1,0:T(8,128)S(1)} %fusion.12) | copy-start | bytes 9437188
  432.5 5.9 collective-permute-start.6
  434.3 14.9 %slice-start.8 = ((s8[4718592]{0:T(1024)(128)(4,1)}), s8[4194304]{0:T(1024)(128)(4,1)S(1)}, s32[]{:S(2)}) async-start(s8[4718592]{0:T(1024)(128)(4,1)} %bitcast.399), calls=%async_computation.20 | async-start | bytes 8388608
  438.5 13.3 %copy-start.36 = (bf16[256,768]{1,0:T(8,128)(2,1)}, bf16[256,768]{1,0:T(8,128)(2,1)S(1)}, u32[]{:S(2)}) copy-start(bf16[256,768]{1,0:T(8,128)(2,1)S(1)} %bitcast_select_fusion) | copy-start | bytes 1179652
  438.5 10.7 %copy-start.16 = (f32[256,768]{1,0:T(8,128)S(1)}, f32[256,768]{1,0:T(8,128)}, u32[]{:S(2)}) copy-start(f32[256,768]{1,0:T(8,128)} %copy-done.15) | copy-start | bytes 2359300
  438.5 10.7 %copy-start.129 = (f32[256]{0:T(256)S(1)}, f32[256]{0:T(256)}, u32[]{:S(2)}) copy-start(f32[256]{0:T(256)} %copy-done.128) | copy-start | bytes 3076
  438.5 10.7 %copy-start.137 = (f32[256]{0:T(256)S(1)}, f32[256]{0:T(256)}, u32[]{:S(2)}) copy-start(f32[256]{0:T(256)} %copy-done.136) | copy-start | bytes 3076
  438.5 10.7 %slice-start.9 = ((s8[4718592]{0:T(1024)(128)(4,1)}), s8[524288]{0:T(1024)(128)(4,1)S(1)}, s32[]{:S(2)}) async-start(s8[4718592]{0:T(1024)(128)(4,1)} %bitcast.399), calls=%async_computation.21 | async-start | bytes 1048576
  461.2 96.9 %reduce-scatter.5.cloned.1.call-start = ((), (), s32[]{:S(2)}) async-start(), calls=%async_computation.4 | async-start | bytes 4423680 | tf_op jit(solution)/shard_map/reduce_scatter | solution.py:233
  474.6 171.2 %reduce-scatter.9.cloned.1.call-start = ((), (), s32[]{:S(2)}) async-start(), calls=%async_computation.6 | async-start | bytes 5898240 | tf_op jit(solution)/shard_map/reduce_scatter | solution.py:245
  490.7 243.2 %reduce-scatter.11.cloned.1.call-start = ((), (), s32[]{:S(2)}) async-start(), calls=%async_computation.7 | async-start | bytes 5898240 | tf_op jit(solution)/shard_map/reduce_scatter | solution.py:248
  491.8 9.7 %copy-start.182 = (f32[256,3072]{1,0:T(8,128)S(1)}, f32[256,3072]{1,0:T(8,128)}, u32[]{:S(2)}) copy-start(f32[256,3072]{1,0:T(8,128)} %copy-done.181) | copy-start | bytes 9437188
  501.5 9.9 %copy-start.37 = (bf16[256,768]{1,0:T(8,128)(2,1)S(1)}, bf16[256,768]{1,0:T(8,128)(2,1)}, u32[]{:S(2)}) copy-start(bf16[256,768]{1,0:T(8,128)(2,1)} %copy-done.36) | copy-start | bytes 1179652
  501.5 9.9 %copy-start.180 = (f32[256,3072]{1,0:T(8,128)S(1)}, f32[256,3072]{1,0:T(8,128)}, u32[]{:S(2)}) copy-start(f32[256,3072]{1,0:T(8,128)} %fusion.8) | copy-start | bytes 9437188
  523.3 309.0 %all-reduce.14.cloned.1.call-start = ((), (), s32[]{:S(2)}) async-start(), calls=%async_computation.11 | async-start | bytes 7077888 | tf_op jit(solution)/shard_map/psum | solution.py:255
  534.7 199.3 %copy-start.40 = (f32[256,768]{1,0:T(8,128)S(1)}, f32[256,768]{1,0:T(8,128)}, u32[]{:S(2)}) copy-start(f32[256,768]{1,0:T(8,128)} %copy-done.39) | copy-start | bytes 2359300
  734.0 16.0 %copy-start.28 = (bf16[256,3,12,64]{0,3,2,1:T(8,128)(2,1)S(1)}, bf16[256,3,12,64]{0,3,2,1:T(8,128)(2,1)}, u32[]{:S(2)}) copy-start(bf16[256,3,12,64]{0,3,2,1:T(8,128)(2,1)} %copy-done.27) | copy-start | bytes 3538948
  734.0 16.0 %copy-start.117 = (f32[256]{0:T(256)S(1)}, f32[256]{0:T(256)}, u32[]{:S(2)}) copy-start(f32[256]{0:T(256)} %copy-done.114) | copy-start | bytes 3076
  750.1 29.6 %copy-start.120 = (f32[256]{0:T(256)S(1)}, f32[256]{0:T(256)}, u32[]{:S(2)}) copy-start(f32[256]{0:T(256)} %copy-done.118) | copy-start | bytes 3076
  750.1 31.1 %copy-start.23 = (f32[256,768]{1,0:T(8,128)S(1)}, f32[256,768]{1,0:T(8,128)}, u32[]{:S(2)}) copy-start(f32[256,768]{1,0:T(8,128)} %copy-done.22) | copy-start | bytes 2359300
  750.1 31.1 %copy-start.38 = (bf16[256,768]{1,0:T(8,128)(2,1)S(1)}, bf16[256,768]{1,0:T(8,128)(2,1)}, u32[]{:S(2)}) copy-start(bf16[256,768]{1,0:T(8,128)(2,1)} %copy-done.36) | copy-start | bytes 1179652
  750.1 31.1 %copy-start.150 = (f32[256]{0:T(256)S(1)}, f32[256]{0:T(256)}, u32[]{:S(2)}) copy-start(f32[256]{0:T(256)} %copy-done.149) | copy-start | bytes 3076
  754.9 26.6 %copy-start.54 = (bf16[1,256,768]{2,1,0:T(8,128)(2,1)S(1)}, bf16[1,256,768]{2,1,0:T(8,128)(2,1)}, u32[]{:S(2)}) copy-start(bf16[1,256,768]{2,1,0:T(8,128)(2,1)} %get-tuple-element.53) | copy-start | bytes 1179652
  (160 other events, 422.4 us)
Sparse Core Ops, SparseCore 0:
  9.6 112.8 all-gather.10
  124.1 42.2 all-gather.12
  167.9 91.6 all-gather.14
  461.3 29.4 reduce-scatter.6
  493.0 65.0 reduce-scatter.4
  560.2 85.5 reduce-scatter.8
  648.1 85.7 reduce-scatter.10
  737.4 94.8 all-reduce.13
